TPU v7x, 32 devices: a whole 2x2x4 slice. The times are simulated.
32 devices in a mesh: dp: 8 (over z, x), shard: 4 (over y, core).
Axes of the slice: x: 2, y: 2, z: 4, core: 2. Of those that a mesh axis runs over, the one named last changes fastest.
Arguments:
- tokens: bfloat16 [8192, 2048], P('dp'), may hold values from -6 to 6
- block_ids: int32 [8, 1024], P('dp'), may hold values from 0 to 7, never falling along the last dimension, each value on 1 to 256 neighbouring positions
- cotangent: bfloat16 [8192, 2048], P('dp'), may hold values from -12 to 12
- gain_first: float32 [2048], P('dp'), may hold values from 0.3 to 2.5
- w_query: float32 [2048, 2048], P('dp', 'shard'), may hold values from -0.125 to 0.125
- w_key: float32 [2048, 512], P('dp', 'shard'), may hold values from -0.125 to 0.125
- w_value: float32 [2048, 512], P('dp', 'shard'), may hold values from -0.125 to 0.125
- w_output: float32 [2048, 2048], P('shard', 'dp'), may hold values from -2 to 2
- gain_second: float32 [2048], P('dp'), may hold values from 0.3 to 2.5
- w_gate: float32 [2048, 8192], P('dp', 'shard'), may hold values from -0.125 to 0.125
- w_up: float32 [2048, 8192], P('dp', 'shard'), may hold values from -0.125 to 0.125
- w_down: float32 [8192, 2048], P('shard', 'dp'), may hold values from -0.0625 to 0.0625
- moment_first: float32 [2048], P('dp'), may hold values from -6 to 6
- moment_query: float32 [2048, 2048], P('dp', 'shard'), may hold values from -4 to 4
- moment_key: float32 [2048, 512], P('dp', 'shard'), may hold values from -4 to 4
- moment_value: float32 [2048, 512], P('dp', 'shard'), may hold values from -4 to 4
- moment_output: float32 [2048, 2048], P('shard', 'dp'), may hold values from -4 to 4
- moment_second: float32 [2048], P('dp'), may hold values from -6 to 6
- moment_gate: float32 [2048, 8192], P('dp', 'shard'), may hold values from -4 to 4
- moment_up: float32 [2048, 8192], P('dp', 'shard'), may hold values from -4 to 4
- moment_down: float32 [8192, 2048], P('shard', 'dp'), may hold values from -4 to 4
- step: int32 [], replicated, may hold values from 1000 to 1999
- rate: float32 [], replicated, may hold values from 0.6 to 1.2
Outputs:
- output: bfloat16 [8192, 2048], P('dp')
- input_grad: float32 [8192, 2048], P('dp')
- global_norm: float32 [], replicated
- momentum_first: float32 [2048], P('dp')
- momentum_query: float32 [2048, 2048], P('dp', 'shard')
- momentum_key: float32 [2048, 512], P('dp', 'shard')
- momentum_value: float32 [2048, 512], P('dp', 'shard')
- momentum_output: float32 [2048, 2048], P('shard', 'dp')
- momentum_second: float32 [2048], P('dp')
- momentum_gate: float32 [2048, 8192], P('dp', 'shard')
- momentum_up: float32 [2048, 8192], P('dp', 'shard')
- momentum_down: float32 [8192, 2048], P('shard', 'dp')
- updated_first: float32 [2048], P('dp')
- updated_query: float32 [2048, 2048], P('dp', 'shard')
- updated_key: float32 [2048, 512], P('dp', 'shard')
- updated_value: float32 [2048, 512], P('dp', 'shard')
- updated_output: float32 [2048, 2048], P('shard', 'dp')
- updated_second: float32 [2048], P('dp')
- updated_gate: float32 [2048, 8192], P('dp', 'shard')
- updated_up: float32 [2048, 8192], P('dp', 'shard')
- updated_down: float32 [8192, 2048], P('shard', 'dp')
Inputs may be any that keep to these rules, and one draw needn't show every extreme that they name: `block_ids`: along each row the block numbers never fall, every number 0 to 7 appears, and a block holds 1 to 256 positions.
All inputs are finite; a program needn't handle non-finite values.
Results may differ from a plain program's by a relative error of at most 0.02.
Values may be sent and summed in bfloat16 or wider, within the bound.
A program may use at most 256 MiB of HBM per device.

v0:
```python
import math
import jax
import jax.numpy as jnp
from jax import lax
from jax.sharding import PartitionSpec as P

H = 32
KV = 8
HD = 64
CLIP = 4096
WARMUP = 2000
EPS = 1e-05
THETA = 10000000.0
NEGATIVE = -1e30


def inverse_rms(values):
    return lax.rsqrt(jnp.mean(values * values, axis=1, keepdims=True) + EPS)


def norm_back(values, inverse, gain, grad_normed):
    scaled = grad_normed * gain[None, :]
    gain_grad = jnp.sum(grad_normed * values * inverse, axis=0)
    grad_values = inverse * scaled - values * inverse**3 * jnp.mean(
        scaled * values, axis=1, keepdims=True
    )
    return (gain_grad, grad_values)


def angle_table(count, length):
    positions = (jnp.arange(count, dtype=jnp.int32) % length).astype(jnp.float32)
    powers = -2.0 * jnp.arange(HD // 2, dtype=jnp.float32) / HD
    angles = positions[:, None] * jnp.power(THETA, powers)[None, :]
    return (jnp.cos(angles)[:, None, :], jnp.sin(angles)[:, None, :])


def rotate(values, cosine, sine):
    half = values.shape[-1] // 2
    first = values[..., :half]
    second = values[..., half:]
    return jnp.concatenate(
        [first * cosine - second * sine, second * cosine + first * sine], axis=-1
    )


def unrotate(grads, cosine, sine):
    half = grads.shape[-1] // 2
    first = grads[..., :half]
    second = grads[..., half:]
    return jnp.concatenate(
        [first * cosine + second * sine, second * cosine - first * sine], axis=-1
    )


def to_items(values, seqs, length):
    shaped = values.reshape((seqs, length) + values.shape[1:])
    moved = jnp.moveaxis(shaped, 2, 1)
    return moved.reshape((seqs * values.shape[1], length) + values.shape[2:])


def from_items(items, seqs):
    groups = items.shape[0] // seqs
    shaped = items.reshape((seqs, groups) + items.shape[1:])
    moved = jnp.moveaxis(shaped, 1, 2)
    return moved.reshape((seqs * items.shape[1], groups) + items.shape[2:])


def item_scores(query, key, blocks, scale):
    scores = jnp.einsum("qgd,jd->gqj", query, key, preferred_element_type=jnp.float32) * scale
    allowed = blocks[None, :] <= blocks[:, None]
    return jnp.where(allowed[None], scores, NEGATIVE)


def attend_forward(scale):

    def run(parts):
        query, key, value, blocks = parts
        scores = item_scores(query, key, blocks, scale)
        peak = jnp.max(scores, axis=2, keepdims=True)
        weights = jnp.exp(scores - peak)
        total = jnp.sum(weights, axis=2, keepdims=True)
        probs = (weights / total).astype(jnp.bfloat16)
        mixed = jnp.einsum("gqj,jd->qgd", probs, value, preferred_element_type=jnp.float32)
        return (mixed.astype(jnp.bfloat16), peak, total)

    return run


def attend_backward(scale):

    def run(parts):
        query, key, value, blocks, peak, total, grad_mixed = parts
        scores = item_scores(query, key, blocks, scale)
        probs = jnp.exp(scores - peak) / total
        probs_low = probs.astype(jnp.bfloat16)
        grad_value = jnp.einsum(
            "gqj,qgd->jd", probs_low, grad_mixed, preferred_element_type=jnp.float32
        )
        grad_probs = jnp.einsum(
            "qgd,jd->gqj", grad_mixed, value, preferred_element_type=jnp.float32
        )
        grad_scores = (
            probs * (grad_probs - jnp.sum(probs * grad_probs, axis=2, keepdims=True))
        ).astype(jnp.bfloat16)
        grad_query = (
            jnp.einsum("gqj,jd->qgd", grad_scores, key, preferred_element_type=jnp.float32) * scale
        )
        grad_key = (
            jnp.einsum("gqj,qgd->jd", grad_scores, query, preferred_element_type=jnp.float32)
            * scale
        )
        return (grad_query, grad_key, grad_value)

    return run


def on_device(
    tokens,
    block_ids,
    cotangent,
    gain_first,
    w_query,
    w_key,
    w_value,
    w_output,
    gain_second,
    w_gate,
    w_up,
    w_down,
    moment_first,
    moment_query,
    moment_key,
    moment_value,
    moment_output,
    moment_second,
    moment_gate,
    moment_up,
    moment_down,
    step,
    rate,
):
    seqs, length = block_ids.shape
    count = tokens.shape[0]
    scale = 1.0 / math.sqrt(HD)
    group = H // KV
    (
        gain_one,
        query_weight,
        key_weight,
        value_weight,
        output_weight,
        gain_two,
        gate_weight,
        up_weight,
        down_weight,
    ) = (
        lax.all_gather(gain_first.astype(jnp.bfloat16), "dp", axis=0, tiled=True),
        lax.all_gather(w_query.astype(jnp.bfloat16), "dp", axis=0, tiled=True),
        lax.all_gather(w_key.astype(jnp.bfloat16), "dp", axis=0, tiled=True),
        lax.all_gather(w_value.astype(jnp.bfloat16), "dp", axis=0, tiled=True),
        lax.all_gather(w_output.astype(jnp.bfloat16), "dp", axis=1, tiled=True),
        lax.all_gather(gain_second.astype(jnp.bfloat16), "dp", axis=0, tiled=True),
        lax.all_gather(w_gate.astype(jnp.bfloat16), "dp", axis=0, tiled=True),
        lax.all_gather(w_up.astype(jnp.bfloat16), "dp", axis=0, tiled=True),
        lax.all_gather(w_down.astype(jnp.bfloat16), "dp", axis=1, tiled=True),
    )
    heads_local = query_weight.shape[1] // HD
    kv_local = key_weight.shape[1] // HD
    inputs = tokens.astype(jnp.float32)
    inverse_first = inverse_rms(inputs)
    gain_one_wide = gain_one.astype(jnp.float32)
    normed = (inputs * inverse_first * gain_one_wide[None, :]).astype(jnp.bfloat16)
    cosine, sine = angle_table(count, length)
    query = rotate(
        jnp.dot(normed, query_weight, preferred_element_type=jnp.float32).reshape(
            count, heads_local, HD
        ),
        cosine,
        sine,
    ).astype(jnp.bfloat16)
    key = rotate(
        jnp.dot(normed, key_weight, preferred_element_type=jnp.float32).reshape(
            count, kv_local, HD
        ),
        cosine,
        sine,
    ).astype(jnp.bfloat16)
    value = (
        jnp.dot(normed, value_weight, preferred_element_type=jnp.float32)
        .astype(jnp.bfloat16)
        .reshape(count, kv_local, HD)
    )
    query_items = to_items(query.reshape(count, kv_local, group, HD), seqs, length)
    key_items = to_items(key, seqs, length)
    value_items = to_items(value, seqs, length)
    block_items = jnp.repeat(block_ids, kv_local, axis=0)
    mixed_items, peak, total = lax.map(
        attend_forward(scale), (query_items, key_items, value_items, block_items)
    )
    mixed = from_items(mixed_items, seqs).reshape(count, heads_local * HD)
    hidden = inputs + lax.psum(
        jnp.dot(mixed, output_weight, preferred_element_type=jnp.float32).astype(jnp.bfloat16),
        "shard",
    ).astype(jnp.float32)
    inverse_second = inverse_rms(hidden)
    gain_two_wide = gain_two.astype(jnp.float32)
    normed_two = (hidden * inverse_second * gain_two_wide[None, :]).astype(jnp.bfloat16)
    gate = jnp.dot(normed_two, gate_weight, preferred_element_type=jnp.float32)
    up = jnp.dot(normed_two, up_weight, preferred_element_type=jnp.float32)
    sigmoid_gate = jax.nn.sigmoid(gate)
    activated = (gate * sigmoid_gate * up).astype(jnp.bfloat16)
    result = hidden + lax.psum(
        jnp.dot(activated, down_weight, preferred_element_type=jnp.float32).astype(jnp.bfloat16),
        "shard",
    ).astype(jnp.float32)
    output = result.astype(jnp.bfloat16)
    grad_result = cotangent.astype(jnp.float32)
    grad_down_weight = jnp.einsum(
        "tf,td->fd", activated, cotangent, preferred_element_type=jnp.float32
    )
    grad_act = jnp.einsum("td,fd->tf", cotangent, down_weight, preferred_element_type=jnp.float32)
    grad_gate_in = (grad_act * up * sigmoid_gate * (1.0 + gate * (1.0 - sigmoid_gate))).astype(
        jnp.bfloat16
    )
    grad_up_in = (grad_act * gate * sigmoid_gate).astype(jnp.bfloat16)
    grad_gate_weight = jnp.einsum(
        "tc,tf->cf", normed_two, grad_gate_in, preferred_element_type=jnp.float32
    )
    grad_up_weight = jnp.einsum(
        "tc,tf->cf", normed_two, grad_up_in, preferred_element_type=jnp.float32
    )
    partial_two = jnp.einsum(
        "tf,cf->tc", grad_gate_in, gate_weight, preferred_element_type=jnp.float32
    ) + jnp.einsum("tf,cf->tc", grad_up_in, up_weight, preferred_element_type=jnp.float32)
    grad_normed_two = lax.psum(partial_two.astype(jnp.bfloat16), "shard").astype(jnp.float32)
    gain_grad_two, grad_through = norm_back(hidden, inverse_second, gain_two_wide, grad_normed_two)
    grad_hidden = grad_result + grad_through
    grad_hidden_low = grad_hidden.astype(jnp.bfloat16)
    grad_output_weight = jnp.einsum(
        "tk,td->kd", mixed, grad_hidden_low, preferred_element_type=jnp.float32
    )
    grad_mixed = jnp.einsum(
        "td,kd->tk", grad_hidden_low, output_weight, preferred_element_type=jnp.float32
    ).astype(jnp.bfloat16)
    grad_mixed_items = to_items(grad_mixed.reshape(count, kv_local, group, HD), seqs, length)
    grad_query_items, grad_key_items, grad_value_items = lax.map(
        attend_backward(scale),
        (query_items, key_items, value_items, block_items, peak, total, grad_mixed_items),
    )
    grad_query_in = (
        unrotate(from_items(grad_query_items, seqs).reshape(count, heads_local, HD), cosine, sine)
        .astype(jnp.bfloat16)
        .reshape(count, heads_local * HD)
    )
    grad_key_in = (
        unrotate(from_items(grad_key_items, seqs), cosine, sine)
        .astype(jnp.bfloat16)
        .reshape(count, kv_local * HD)
    )
    grad_value_in = (
        from_items(grad_value_items, seqs).astype(jnp.bfloat16).reshape(count, kv_local * HD)
    )
    grad_query_weight = jnp.einsum(
        "tc,tk->ck", normed, grad_query_in, preferred_element_type=jnp.float32
    )
    grad_key_weight = jnp.einsum(
        "tc,tk->ck", normed, grad_key_in, preferred_element_type=jnp.float32
    )
    grad_value_weight = jnp.einsum(
        "tc,tk->ck", normed, grad_value_in, preferred_element_type=jnp.float32
    )
    partial_one = jnp.einsum(
        "tk,ck->tc", grad_query_in, query_weight, preferred_element_type=jnp.float32
    )
    partial_one = partial_one + jnp.einsum(
        "tk,ck->tc", grad_key_in, key_weight, preferred_element_type=jnp.float32
    )
    partial_one = partial_one + jnp.einsum(
        "tk,ck->tc", grad_value_in, value_weight, preferred_element_type=jnp.float32
    )
    grad_normed = lax.psum(partial_one.astype(jnp.bfloat16), "shard").astype(jnp.float32)
    gain_grad_one, grad_inner = norm_back(inputs, inverse_first, gain_one_wide, grad_normed)
    input_grad = grad_hidden + grad_inner
    owned = (
        lax.psum_scatter(
            gain_grad_one.astype(jnp.bfloat16), "dp", scatter_dimension=0, tiled=True
        ).astype(jnp.float32),
        lax.psum_scatter(
            grad_query_weight.astype(jnp.bfloat16), "dp", scatter_dimension=0, tiled=True
        ).astype(jnp.float32),
        lax.psum_scatter(
            grad_key_weight.astype(jnp.bfloat16), "dp", scatter_dimension=0, tiled=True
        ).astype(jnp.float32),
        lax.psum_scatter(
            grad_value_weight.astype(jnp.bfloat16), "dp", scatter_dimension=0, tiled=True
        ).astype(jnp.float32),
        lax.psum_scatter(
            grad_output_weight.astype(jnp.bfloat16), "dp", scatter_dimension=1, tiled=True
        ).astype(jnp.float32),
        lax.psum_scatter(
            gain_grad_two.astype(jnp.bfloat16), "dp", scatter_dimension=0, tiled=True
        ).astype(jnp.float32),
        lax.psum_scatter(
            grad_gate_weight.astype(jnp.bfloat16), "dp", scatter_dimension=0, tiled=True
        ).astype(jnp.float32),
        lax.psum_scatter(
            grad_up_weight.astype(jnp.bfloat16), "dp", scatter_dimension=0, tiled=True
        ).astype(jnp.float32),
        lax.psum_scatter(
            grad_down_weight.astype(jnp.bfloat16), "dp", scatter_dimension=1, tiled=True
        ).astype(jnp.float32),
    )
    first_shard = (lax.axis_index("shard") == 0).astype(jnp.float32)
    squares = first_shard * (jnp.sum(owned[0] * owned[0]) + jnp.sum(owned[5] * owned[5]))
    for position in (1, 2, 3, 4, 6, 7, 8):
        squares = squares + jnp.sum(owned[position] * owned[position])
    global_norm = jnp.sqrt(lax.psum(squares, ("dp", "shard")))
    factor = jnp.minimum(1.0, CLIP / global_norm)
    rate_now = rate * jnp.minimum(1.0, (step.astype(jnp.float32) + 1.0) / WARMUP)
    masters = (gain_first, w_query, w_key, w_value, w_output, gain_second, w_gate, w_up, w_down)
    moments = (
        moment_first,
        moment_query,
        moment_key,
        moment_value,
        moment_output,
        moment_second,
        moment_gate,
        moment_up,
        moment_down,
    )
    momenta = [0.5 * moment + 0.5 * (factor * gradient) for moment, gradient in zip(moments, owned)]
    updated = [master - rate_now * momentum for master, momentum in zip(masters, momenta)]
    return (
        output,
        input_grad,
        global_norm,
        momenta[0],
        momenta[1],
        momenta[2],
        momenta[3],
        momenta[4],
        momenta[5],
        momenta[6],
        momenta[7],
        momenta[8],
        updated[0],
        updated[1],
        updated[2],
        updated[3],
        updated[4],
        updated[5],
        updated[6],
        updated[7],
        updated[8],
    )


def solution(mesh):
    in_specs = (
        P("dp", None),
        P("dp", None),
        P("dp", None),
        P("dp"),
        P("dp", "shard"),
        P("dp", "shard"),
        P("dp", "shard"),
        P("shard", "dp"),
        P("dp"),
        P("dp", "shard"),
        P("dp", "shard"),
        P("shard", "dp"),
        P("dp"),
        P("dp", "shard"),
        P("dp", "shard"),
        P("dp", "shard"),
        P("shard", "dp"),
        P("dp"),
        P("dp", "shard"),
        P("dp", "shard"),
        P("shard", "dp"),
        P(),
        P(),
    )
    out_specs = (
        P("dp", None),
        P("dp", None),
        P(),
        P("dp"),
        P("dp", "shard"),
        P("dp", "shard"),
        P("dp", "shard"),
        P("shard", "dp"),
        P("dp"),
        P("dp", "shard"),
        P("dp", "shard"),
        P("shard", "dp"),
        P("dp"),
        P("dp", "shard"),
        P("dp", "shard"),
        P("dp", "shard"),
        P("shard", "dp"),
        P("dp"),
        P("dp", "shard"),
        P("dp", "shard"),
        P("shard", "dp"),
    )
    return jax.shard_map(
        on_device, mesh=mesh, in_specs=in_specs, out_specs=out_specs, check_vma=False
    )
```

profile of v0, /device:TPU:0, one launch (start us, length us, event | category | flops | bytes accessed | tf_op | source)
XLA Modules:
  0.0 1819.1 jit_solution(10321602777745166804)
XLA Ops:
  11.8 22.4 %all-gather = bf16[8,1,256]{2,1,0:T(2,128)(2,1)S(1)} all-gather(bf16[1,1,256]{2,1,0:T(2,128)(2,1)S(1)} %reshape.331), channel_id=1, replica_groups=mesh['dp'=8,'shard'=4] {'dp'}, dimensions={0}, use_global_device_ids=true | all-gather | bytes 4608 | tf_op jit(solution)/shard_map/all_gather | solution.py:157
  38.9 32.9 %all_gather.28 = bf16[2048,128]{1,0:T(8,128)(2,1)S(1)} all-gather(bf16[256,128]{1,0:T(8,128)(2,1)S(1)} %convert_element_type.243), channel_id=1, replica_groups=mesh['dp'=8,'shard'=4] {'dp'}, dimensions={0}, use_global_device_ids=true | all-gather | bytes 589824 | tf_op jit(solution)/shard_map/all_gather | solution.py:160
  72.8 31.7 %all_gather.29 = bf16[2048,128]{1,0:T(8,128)(2,1)S(1)} all-gather(bf16[256,128]{1,0:T(8,128)(2,1)S(1)} %convert_element_type.245), channel_id=1, replica_groups=mesh['dp'=8,'shard'=4] {'dp'}, dimensions={0}, use_global_device_ids=true | all-gather | bytes 589824 | tf_op jit(solution)/shard_map/all_gather | solution.py:159
  116.8 30.4 %while.28 = (s32[]{:T(128)}, bf16[2,1024,4,64]{1,3,2,0:T(8,128)(2,1)}, f32[2,4,1024,1]{2,1,3,0:T(4,128)}, f32[2,4,1024,1]{2,1,3,0:T(4,128)}, bf16[2,1024,64]{1,2...) while((s32[]{:T(128)}, ...), condition=%wide.region_4.5_spmd, body=%wide.region_1.4_spmd.sunk | while | flops 1125376000 | bytes 64387236 | solution.py:197
  160.8 16.6 all-gather.1
  177.3 59.9 %all-reduce.8.cloned.1.call-done = bf16[1024,2048]{1,0:T(8,128)(2,1)} async-done(((bf16[1024,2048]{1,0:T(8,128)(2,1)}), bf16[1024,2048]{1,0:T(8,128)(2,1)}) %all-reduce.8.cloned.1.call-update) | async-done | bytes 4194320 | tf_op jit(solution)/shard_map/psum | solution.py:201
  247.8 117.3 %all-gather.12.cloned.1.call-done = bf16[2048,2048]{1,0:T(8,128)(2,1)} async-done(((bf16[256,2048]{1,0:T(8,128)(2,1)}), bf16[2048,2048]{1,0:T(8,128)(2,1)}) %all-gather.12.cloned.1.call-update) | async-done | bytes 8388624 | tf_op jit(solution)/shard_map/all_gather | solution.py:163
  365.1 14.5 fusion.112
  379.6 111.4 %all-gather.14.cloned.1.call-done = bf16[2048,2048]{1,0:T(8,128)(2,1)} async-done(((bf16[256,2048]{1,0:T(8,128)(2,1)}), bf16[2048,2048]{1,0:T(8,128)(2,1)}) %all-gather.14.cloned.1.call-update) | async-done | bytes 8388624 | tf_op jit(solution)/shard_map/all_gather | solution.py:164
  491.0 14.5 fusion.113
  505.5 111.8 %all-gather.16.cloned.1.call-done = bf16[2048,2048]{1,0:T(8,128)(2,1)} async-done(((bf16[2048,256]{1,0:T(8,128)(2,1)}), bf16[2048,2048]{1,0:T(8,128)(2,1)}) %all-gather.16.cloned.1.call-update) | async-done | bytes 8388624 | tf_op jit(solution)/shard_map/all_gather | solution.py:165
  617.3 22.1 %multiply_convert_fusion = (bf16[1024,2048]{1,0:T(8,128)(2,1)}, bf16[1024,2048]{1,0:T(8,128)(2,1)}, bf16[1024,2048]{1,0:T(8,128)(2,1)}) fusion(f32[1024,2048]{1,0:T(8,128)} %fusion.112, f32[1024,2048]{1,0:T(8,128)} %fusion.113, bf16[1024,2048]{1,0:T(8,128)(2,1)} %param.29, bf16[2048,2048]{1,0:T(8,128)(2,1)} %all-gather.16.cloned.1.call-done), kind=kOutput, calls=%fused_computation.96 | convolution fusion | flops 8623489024 | bytes 41943040 | tf_op jit(solution)/shard_map/td,fd->tf/dot_general | solution.py:221
  639.4 14.7 fusion.114
  654.1 12.2 add_convert_fusion.1
  666.4 83.8 %all-reduce.10.cloned.1.call-done = bf16[1024,2048]{1,0:T(8,128)(2,1)} async-done(((bf16[1024,2048]{1,0:T(8,128)(2,1)}), bf16[1024,2048]{1,0:T(8,128)(2,1)}) %all-reduce.10.cloned.1.call-update) | async-done | bytes 4194320 | tf_op jit(solution)/shard_map/psum | solution.py:235
  767.5 79.0 %while.29 = (s32[]{:T(128)}, f32[2,1024,4,64]{1,3,2,0:T(8,128)}, f32[2,1024,64]{1,2,0:T(8,128)}, bf16[2,1024,64]{1,2,0:T(8,128)(2,1)}, bf16[2,1024,64]{1,2,0:T(8...) while((s32[]{:T(128)}, f32[2,1024,4,64]{1,3,2,0:T(8,128)}, ...), condition=%wide.region_12.13_spmd, body=%wide.region_10.12_spmd.sunk | while | flops 2727669760 | bytes 159401328 | solution.py:246
  778.4 11.7 fusion.190
  817.8 11.7 fusion.190
  852.1 13.9 convolution_convert_fusion.3
  890.8 14.0 convolution_convert_fusion.2
  905.3 14.1 convolution_convert_fusion.1
  919.4 14.1 convolution_convert_fusion
  937.6 41.8 %reduce-scatter.12.cloned.1.call-done = bf16[256,128]{1,0:T(8,128)(2,1)} async-done(((bf16[2048,128]{1,0:T(8,128)(2,1)}), bf16[256,128]{1,0:T(8,128)(2,1)}) %reduce-scatter.12.cloned.1.call-update) | async-done | bytes 65552 | tf_op jit(solution)/shard_map/reduce_scatter | solution.py:294
  980.9 153.2 %all-reduce.12.cloned.1.call-done = (bf16[1024,2048]{1,0:T(8,128)(2,1)}, bf16[1024,2048]{1,0:T(8,128)(2,1)}) async-done(((bf16[1024,2048]{1,0:T(8,128)(2,1)}, bf16[1024,2048]{1,0:T(8,128)(2,1)}), (bf16[1024,2048]{1,0:T(8,128)(2,1)}, bf16[1024,2048]{1,0:T(8,128)(2,1)})) %all-reduce.12.cloned.1.call-update) | async-done | bytes 8388624 | tf_op jit(solution)/shard_map/psum | solution.py:212
  1139.8 22.3 %all-reduce.2 = (bf16[2048]{0:T(1024)(128)(2,1)S(1)}, bf16[2048]{0:T(1024)(128)(2,1)S(1)}) all-reduce(bf16[2048]{0:T(1024)(128)(2,1)S(1)} %get-tuple-element.132, bf16[2048]{0:T(1024)(128)(2,1)S(1)} %copy-done.43), channel_id=2, replica_groups=mesh['dp'=8,'shard'=4] {'dp'}, use_global_device_ids=true, to_apply=%region_16.17.clone | all-reduce | flops 4096 | bytes 16384
  1164.1 41.8 %reduce-scatter.8.cloned.1.call-done = bf16[256,512]{1,0:T(8,128)(2,1)} async-done(((bf16[2048,512]{1,0:T(8,128)(2,1)}), bf16[256,512]{1,0:T(8,128)(2,1)}) %reduce-scatter.8.cloned.1.call-update) | async-done | bytes 262160 | tf_op jit(solution)/shard_map/reduce_scatter | solution.py:288
  1209.5 67.7 %reduce-scatter.14.cloned.1.call-done = bf16[512,256]{1,0:T(8,128)(2,1)} async-done(((bf16[512,2048]{1,0:T(8,128)(2,1)}), bf16[512,256]{1,0:T(8,128)(2,1)}) %reduce-scatter.14.cloned.1.call-update) | async-done | bytes 262160 | tf_op jit(solution)/shard_map/reduce_scatter | solution.py:297
  1280.1 148.8 %reduce-scatter.16.cloned.1.call-done = bf16[256,2048]{1,0:T(8,128)(2,1)} async-done(((bf16[2048,2048]{1,0:T(8,128)(2,1)}), bf16[256,2048]{1,0:T(8,128)(2,1)}) %reduce-scatter.16.cloned.1.call-update) | async-done | bytes 1048592 | tf_op jit(solution)/shard_map/reduce_scatter | solution.py:303
  1431.9 148.9 %reduce-scatter.18.cloned.1.call-done = bf16[256,2048]{1,0:T(8,128)(2,1)} async-done(((bf16[2048,2048]{1,0:T(8,128)(2,1)}), bf16[256,2048]{1,0:T(8,128)(2,1)}) %reduce-scatter.18.cloned.1.call-update) | async-done | bytes 1048592 | tf_op jit(solution)/shard_map/reduce_scatter | solution.py:306
  1583.9 148.9 %reduce-scatter.20.cloned.1.call-done = bf16[2048,256]{1,0:T(8,128)(2,1)} async-done(((bf16[2048,2048]{1,0:T(8,128)(2,1)}), bf16[2048,256]{1,0:T(8,128)(2,1)}) %reduce-scatter.20.cloned.1.call-update) | async-done | bytes 1048592 | tf_op jit(solution)/shard_map/reduce_scatter | solution.py:309
  1735.9 14.7 fusion.60
  1750.7 39.0 %psum.39 = f32[]{:T(128)} all-reduce(f32[]{:T(128)S(6)} %add.221), channel_id=1, replica_groups=mesh['dp'=8,'shard'=4] {'dp','shard'}, use_global_device_ids=true, to_apply=%region_35.36 | all-reduce | flops 1 | bytes 8 | tf_op jit(solution)/shard_map/psum | solution.py:317
  (261 shorter events, 221.2 us)
Async XLA Ops:
  7.2 103.3 %all-gather.8.cloned.1.call-start = ((), (), s32[]{:S(2)}) async-start(), calls=%async_computation.7 | async-start | bytes 2359296 | tf_op jit(solution)/shard_map/all_gather | solution.py:158
  9.0 138.2 %all-gather.10.cloned.1.call-start = ((), (), s32[]{:S(2)}) async-start(), calls=%async_computation.8 | async-start | bytes 2359296 | tf_op jit(solution)/shard_map/all_gather | solution.py:161
  10.9 226.4 %all-reduce.8.cloned.1.call-start = ((), (), s32[]{:S(2)}) async-start(), calls=%async_computation.9 | async-start | bytes 8388608 | tf_op jit(solution)/shard_map/psum | solution.py:201
  11.0 93.5 %copy-start = (bf16[1024,2048]{1,0:T(8,128)(2,1)S(1)}, bf16[1024,2048]{1,0:T(8,128)(2,1)}, u32[]{:S(2)}) copy-start(bf16[1024,2048]{1,0:T(8,128)(2,1)} %param.27) | copy-start | bytes 12582916
  34.3 72.8 %copy-start.38 = (f32[8,1,256]{2,1,0:T(1,128)}, f32[8,1,256]{2,1,0:T(1,128)S(1)}, u32[]{:S(2)}) copy-start(f32[8,1,256]{2,1,0:T(1,128)S(1)} %convert_element_type.295) | copy-start | bytes 24580
  38.0 71.1 %copy-start.40 = (f32[1024]{0:T(1024)}, f32[1024]{0:T(1024)S(1)}, u32[]{:S(2)}) copy-start(f32[1024]{0:T(1024)S(1)} %get-tuple-element.218) | copy-start | bytes 12292
  71.7 37.3 %copy-start.15 = (bf16[2048,128]{1,0:T(8,128)(2,1)}, bf16[2048,128]{1,0:T(8,128)(2,1)S(1)}, u32[]{:S(2)}) copy-start(bf16[2048,128]{1,0:T(8,128)(2,1)S(1)} %all_gather.28) | copy-start | bytes 1572868
  154.0 211.2 %all-gather.12.cloned.1.call-start = ((), (), s32[]{:S(2)}) async-start(), calls=%async_computation.10 | async-start | bytes 9437184 | tf_op jit(solution)/shard_map/all_gather | solution.py:163
  155.2 335.8 %all-gather.14.cloned.1.call-start = ((), (), s32[]{:S(2)}) async-start(), calls=%async_computation.11 | async-start | bytes 9437184 | tf_op jit(solution)/shard_map/all_gather | solution.py:164
  157.9 459.3 %all-gather.16.cloned.1.call-start = ((), (), s32[]{:S(2)}) async-start(), calls=%async_computation.12 | async-start | bytes 9437184 | tf_op jit(solution)/shard_map/all_gather | solution.py:165
  160.7 589.4 %all-reduce.10.cloned.1.call-start = ((), (), s32[]{:S(2)}) async-start(), calls=%async_computation.13 | async-start | bytes 8388608 | tf_op jit(solution)/shard_map/psum | solution.py:235
  666.3 269.8 %reduce-scatter.10.cloned.1.call-start = ((), (), s32[]{:S(2)}) async-start(), calls=%async_computation.15 | async-start | bytes 589824 | tf_op jit(solution)/shard_map/reduce_scatter | solution.py:291
  767.5 79.0 %copy-start.23 = (f32[1024,32]{0,1:T(8,128)S(1)}, f32[1024,32]{0,1:T(8,128)}, u32[]{:S(2)}) copy-start(f32[1024,32]{0,1:T(8,128)} %copy-done.22) | copy-start | bytes 393220
  767.5 79.0 %copy-start.25 = (f32[1024,32]{0,1:T(8,128)S(1)}, f32[1024,32]{0,1:T(8,128)}, u32[]{:S(2)}) copy-start(f32[1024,32]{0,1:T(8,128)} %copy-done.24) | copy-start | bytes 393220
  852.0 127.5 %reduce-scatter.12.cloned.1.call-start = ((), (), s32[]{:S(2)}) async-start(), calls=%async_computation.16 | async-start | bytes 589824 | tf_op jit(solution)/shard_map/reduce_scatter | solution.py:294
  868.6 265.5 %all-reduce.12.cloned.1.call-start = ((), (), s32[]{:S(2)}) async-start(), calls=%async_computation.21 | async-start | bytes 16777216 | tf_op jit(solution)/shard_map/psum | solution.py:212
  877.3 328.6 %reduce-scatter.8.cloned.1.call-start = ((), (), s32[]{:S(2)}) async-start(), calls=%async_computation.14 | async-start | bytes 2359296 | tf_op jit(solution)/shard_map/reduce_scatter | solution.py:288
  883.6 393.6 %reduce-scatter.14.cloned.1.call-start = ((), (), s32[]{:S(2)}) async-start(), calls=%async_computation.17 | async-start | bytes 2359296 | tf_op jit(solution)/shard_map/reduce_scatter | solution.py:297
  890.7 538.2 %reduce-scatter.16.cloned.1.call-start = ((), (), s32[]{:S(2)}) async-start(), calls=%async_computation.18 | async-start | bytes 9437184 | tf_op jit(solution)/shard_map/reduce_scatter | solution.py:303
  904.8 676.1 %reduce-scatter.18.cloned.1.call-start = ((), (), s32[]{:S(2)}) async-start(), calls=%async_computation.19 | async-start | bytes 9437184 | tf_op jit(solution)/shard_map/reduce_scatter | solution.py:306
  919.4 813.5 %reduce-scatter.20.cloned.1.call-start = ((), (), s32[]{:S(2)}) async-start(), calls=%async_computation.20 | async-start | bytes 9437184 | tf_op jit(solution)/shard_map/reduce_scatter | solution.py:309
  933.5 200.6 %copy-start.39 = (f32[8,1,256]{2,1,0:T(1,128)S(1)}, f32[8,1,256]{2,1,0:T(1,128)}, u32[]{:S(2)}) copy-start(f32[8,1,256]{2,1,0:T(1,128)} %copy-done.38) | copy-start | bytes 24580
  933.5 200.6 %copy-start.41 = (f32[1024]{0:T(1024)S(1)}, f32[1024]{0:T(1024)}, u32[]{:S(2)}) copy-start(f32[1024]{0:T(1024)} %copy-done.40) | copy-start | bytes 12292
  933.5 206.3 %copy-start.43 = (bf16[2048]{0:T(1024)(128)(2,1)S(1)}, bf16[2048]{0:T(1024)(128)(2,1)}, u32[]{:S(2)}) copy-start(bf16[2048]{0:T(1024)(128)(2,1)} %get-tuple-element.130) | copy-start | bytes 12292
  933.5 802.4 %copy-start.42 = (f32[1024]{0:T(1024)S(1)}, f32[1024]{0:T(1024)}, u32[]{:S(2)}) copy-start(f32[1024]{0:T(1024)} %get-tuple-element.217) | copy-start | bytes 12292
  1162.1 573.8 %copy-start.46 = (bf16[2048]{0:T(1024)(128)(2,1)}, bf16[2048]{0:T(1024)(128)(2,1)S(1)}, u32[]{:S(2)}) copy-start(bf16[2048]{0:T(1024)(128)(2,1)S(1)} %get-tuple-element.173) | copy-start | bytes 12292
  1162.1 573.8 %copy-start.47 = (bf16[2048]{0:T(1024)(128)(2,1)}, bf16[2048]{0:T(1024)(128)(2,1)S(1)}, u32[]{:S(2)}) copy-start(bf16[2048]{0:T(1024)(128)(2,1)S(1)} %get-tuple-element.172) | copy-start | bytes 12292
  1735.9 57.5 %copy-start.31 = (bf16[256,512]{1,0:T(8,128)(2,1)S(1)}, bf16[256,512]{1,0:T(8,128)(2,1)}, u32[]{:S(2)}) copy-start(bf16[256,512]{1,0:T(8,128)(2,1)} %reduce-scatter.8.cloned.1.call-done) | copy-start | bytes 786436
  1735.9 59.9 %copy-start.34 = (f32[256,128]{1,0:T(8,128)S(1)}, f32[256,128]{1,0:T(8,128)}, u32[]{:S(2)}) copy-start(f32[256,128]{1,0:T(8,128)} %param.32) | copy-start | bytes 393220
  1735.9 65.5 %copy-start.12 = (f32[256,2048]{1,0:T(8,128)S(1)}, f32[256,2048]{1,0:T(8,128)}, u32[]{:S(2)}) copy-start(f32[256,2048]{1,0:T(8,128)} %param.36) | copy-start | bytes 6291460
  1735.9 65.5 %copy-start.19 = (bf16[256,2048]{1,0:T(8,128)(2,1)S(1)}, bf16[256,2048]{1,0:T(8,128)(2,1)}, u32[]{:S(2)}) copy-start(bf16[256,2048]{1,0:T(8,128)(2,1)} %reduce-scatter.16.cloned.1.call-done) | copy-start | bytes 3145732
  1790.5 15.5 copy-start.13
  (47 other events, 296.8 us)
Sparse Core Ops, SparseCore 0:
  10.7 58.7 all-gather.7
  72.2 52.4 all-gather.9
  154.1 83.1 all-reduce.7
  240.0 125.0 all-gather.11
  367.9 123.0 all-gather.13
  493.7 123.5 all-gather.15
  666.4 83.6 all-reduce.9
  852.1 62.0 reduce-scatter.9
  918.5 60.9 reduce-scatter.11
  981.9 152.2 all-reduce.11
  1138.2 67.5 reduce-scatter.7
  1209.8 67.3 reduce-scatter.13
  1280.8 148.0 reduce-scatter.15
  1432.8 148.0 reduce-scatter.17
  1584.4 148.4 reduce-scatter.19
where the time goes:
time: 1830 us; the launch traced here: 1820 us
  waiting for transfers between devices  1240 us (68%)
  matrix products  253 us (14%)
  blocking collectives  165 us (9%)
  other arithmetic  126 us (7%)
  between operations  24.5 us (1%)
    psum x1, waiting for transfers between devices, on_device(): lax.psum(jnp.dot(activated, down_weight, preferred_element_type=jnp.float...  153 us
    reduce_scatter x1, waiting for transfers between devices, on_device(): lax.psum_scatter(grad_up_weight.astype(jnp.bfloat16), 'dp', scatter_dimen...  149 us
    reduce_scatter x1, waiting for transfers between devices, on_device(): lax.psum_scatter(grad_down_weight.astype(jnp.bfloat16), 'dp', scatter_dim...  149 us
    reduce_scatter x1, waiting for transfers between devices, on_device(): lax.psum_scatter(grad_gate_weight.astype(jnp.bfloat16), 'dp', scatter_dim...  149 us
    all_gather x1, waiting for transfers between devices, on_device(): lax.all_gather(w_gate.astype(jnp.bfloat16), 'dp', axis=0, tiled=True)  117 us
    all_gather x1, waiting for transfers between devices, on_device(): lax.all_gather(w_down.astype(jnp.bfloat16), 'dp', axis=1, tiled=True)  112 us
    all_gather x1, waiting for transfers between devices, on_device(): lax.all_gather(w_up.astype(jnp.bfloat16), 'dp', axis=0, tiled=True)  111 us
    psum x1, waiting for transfers between devices, on_device(): lax.psum(partial_two.astype(jnp.bfloat16), 'shard').astype(jnp.float32)  83.8 us
  transfers between devices with their start and end apart: 15, of which 12 were waited for; matrix products, arithmetic and copies ran while one was open for 11% of the time, Pallas kernels for 0%

commit v1 on v0

--- a/solution.py
+++ b/solution.py
@@ -314,7 +314,7 @@
     squares = first_shard * (jnp.sum(owned[0] * owned[0]) + jnp.sum(owned[5] * owned[5]))
     for position in (1, 2, 3, 4, 6, 7, 8):
         squares = squares + jnp.sum(owned[position] * owned[position])
-    global_norm = jnp.sqrt(lax.psum(squares, ("dp", "shard")))
+    global_norm = jnp.sqrt(lax.psum(lax.psum(squares, "shard"), "dp"))
     factor = jnp.minimum(1.0, CLIP / global_norm)
     rate_now = rate * jnp.minimum(1.0, (step.astype(jnp.float32) + 1.0) / WARMUP)
     masters = (gain_first, w_query, w_key, w_value, w_output, gain_second, w_gate, w_up, w_down)

time: 1830 us -> 1820 us (level)
    psum x1 -> x2, blocking collectives: 39 us -> 27.4 us  [on_device(): global_norm = jnp.sqrt(lax.psum(lax.psum(squares, 'shard'), 'dp'))]
where the time goes in v1:
time: 1820 us; the launch traced here: 1810 us
  waiting for transfers between devices  1240 us (68%)
  matrix products  253 us (14%)
  blocking collectives  153 us (8%)
  other arithmetic  126 us (7%)
  between operations  24.5 us (1%)
    psum x1, waiting for transfers between devices, on_device(): lax.psum(jnp.dot(activated, down_weight, preferred_element_type=jnp.float...  153 us
    reduce_scatter x1, waiting for transfers between devices, on_device(): lax.psum_scatter(grad_gate_weight.astype(jnp.bfloat16), 'dp', scatter_dim...  149 us
    reduce_scatter x1, waiting for transfers between devices, on_device(): lax.psum_scatter(grad_up_weight.astype(jnp.bfloat16), 'dp', scatter_dimen...  149 us
    reduce_scatter x1, waiting for transfers between devices, on_device(): lax.psum_scatter(grad_down_weight.astype(jnp.bfloat16), 'dp', scatter_dim...  149 us
    all_gather x1, waiting for transfers between devices, on_device(): lax.all_gather(w_gate.astype(jnp.bfloat16), 'dp', axis=0, tiled=True)  117 us
    all_gather x1, waiting for transfers between devices, on_device(): lax.all_gather(w_down.astype(jnp.bfloat16), 'dp', axis=1, tiled=True)  112 us
    all_gather x1, waiting for transfers between devices, on_device(): lax.all_gather(w_up.astype(jnp.bfloat16), 'dp', axis=0, tiled=True)  111 us
    psum x1, waiting for transfers between devices, on_device(): lax.psum(partial_two.astype(jnp.bfloat16), 'shard').astype(jnp.float32)  83.8 us
  transfers between devices with their start and end apart: 15, of which 12 were waited for; matrix products, arithmetic and copies ran while one was open for 11% of the time, Pallas kernels for 0%

profile of v1, /device:TPU:0, one launch (start us, length us, event | category | flops | bytes accessed | tf_op | source)
XLA Modules:
  0.0 1807.8 jit_solution(323876094008166666)
XLA Ops:
  11.8 22.4 %all-gather = bf16[8,1,256]{2,1,0:T(2,128)(2,1)S(1)} all-gather(bf16[1,1,256]{2,1,0:T(2,128)(2,1)S(1)} %reshape.331), channel_id=1, replica_groups=mesh['dp'=8,'shard'=4] {'dp'}, dimensions={0}, use_global_device_ids=true | all-gather | bytes 4608 | tf_op jit(solution)/shard_map/all_gather | solution.py:157
  38.9 32.9 %all_gather.28 = bf16[2048,128]{1,0:T(8,128)(2,1)S(1)} all-gather(bf16[256,128]{1,0:T(8,128)(2,1)S(1)} %convert_element_type.243), channel_id=1, replica_groups=mesh['dp'=8,'shard'=4] {'dp'}, dimensions={0}, use_global_device_ids=true | all-gather | bytes 589824 | tf_op jit(solution)/shard_map/all_gather | solution.py:160
  72.8 31.9 %all_gather.29 = bf16[2048,128]{1,0:T(8,128)(2,1)S(1)} all-gather(bf16[256,128]{1,0:T(8,128)(2,1)S(1)} %convert_element_type.245), channel_id=1, replica_groups=mesh['dp'=8,'shard'=4] {'dp'}, dimensions={0}, use_global_device_ids=true | all-gather | bytes 589824 | tf_op jit(solution)/shard_map/all_gather | solution.py:159
  116.9 30.4 %while.28 = (s32[]{:T(128)}, bf16[2,1024,4,64]{1,3,2,0:T(8,128)(2,1)}, f32[2,4,1024,1]{2,1,3,0:T(4,128)}, f32[2,4,1024,1]{2,1,3,0:T(4,128)}, bf16[2,1024,64]{1,2...) while((s32[]{:T(128)}, ...), condition=%wide.region_4.5_spmd, body=%wide.region_1.4_spmd.sunk | while | flops 1125376000 | bytes 64387236 | solution.py:197
  161.0 16.3 all-gather.1
  177.3 59.8 %all-reduce.8.cloned.1.call-done = bf16[1024,2048]{1,0:T(8,128)(2,1)} async-done(((bf16[1024,2048]{1,0:T(8,128)(2,1)}), bf16[1024,2048]{1,0:T(8,128)(2,1)}) %all-reduce.8.cloned.1.call-update) | async-done | bytes 4194320 | tf_op jit(solution)/shard_map/psum | solution.py:201
  247.6 117.3 %all-gather.12.cloned.1.call-done = bf16[2048,2048]{1,0:T(8,128)(2,1)} async-done(((bf16[256,2048]{1,0:T(8,128)(2,1)}), bf16[2048,2048]{1,0:T(8,128)(2,1)}) %all-gather.12.cloned.1.call-update) | async-done | bytes 8388624 | tf_op jit(solution)/shard_map/all_gather | solution.py:163
  364.9 14.5 fusion.112
  379.4 111.4 %all-gather.14.cloned.1.call-done = bf16[2048,2048]{1,0:T(8,128)(2,1)} async-done(((bf16[256,2048]{1,0:T(8,128)(2,1)}), bf16[2048,2048]{1,0:T(8,128)(2,1)}) %all-gather.14.cloned.1.call-update) | async-done | bytes 8388624 | tf_op jit(solution)/shard_map/all_gather | solution.py:164
  490.8 14.4 fusion.113
  505.2 111.9 %all-gather.16.cloned.1.call-done = bf16[2048,2048]{1,0:T(8,128)(2,1)} async-done(((bf16[2048,256]{1,0:T(8,128)(2,1)}), bf16[2048,2048]{1,0:T(8,128)(2,1)}) %all-gather.16.cloned.1.call-update) | async-done | bytes 8388624 | tf_op jit(solution)/shard_map/all_gather | solution.py:165
  617.1 22.1 %multiply_convert_fusion = (bf16[1024,2048]{1,0:T(8,128)(2,1)}, bf16[1024,2048]{1,0:T(8,128)(2,1)}, bf16[1024,2048]{1,0:T(8,128)(2,1)}) fusion(f32[1024,2048]{1,0:T(8,128)} %fusion.112, f32[1024,2048]{1,0:T(8,128)} %fusion.113, bf16[1024,2048]{1,0:T(8,128)(2,1)} %param.29, bf16[2048,2048]{1,0:T(8,128)(2,1)} %all-gather.16.cloned.1.call-done), kind=kOutput, calls=%fused_computation.96 | convolution fusion | flops 8623489024 | bytes 41943040 | tf_op jit(solution)/shard_map/td,fd->tf/dot_general | solution.py:221
  639.1 14.7 fusion.114
  653.8 12.2 add_convert_fusion.1
  666.2 83.8 %all-reduce.10.cloned.1.call-done = bf16[1024,2048]{1,0:T(8,128)(2,1)} async-done(((bf16[1024,2048]{1,0:T(8,128)(2,1)}), bf16[1024,2048]{1,0:T(8,128)(2,1)}) %all-reduce.10.cloned.1.call-update) | async-done | bytes 4194320 | tf_op jit(solution)/shard_map/psum | solution.py:235
  767.4 78.9 %while.29 = (s32[]{:T(128)}, f32[2,1024,4,64]{1,3,2,0:T(8,128)}, f32[2,1024,64]{1,2,0:T(8,128)}, bf16[2,1024,64]{1,2,0:T(8,128)(2,1)}, bf16[2,1024,64]{1,2,0:T(8...) while((s32[]{:T(128)}, f32[2,1024,4,64]{1,3,2,0:T(8,128)}, ...), condition=%wide.region_12.13_spmd, body=%wide.region_10.12_spmd.sunk | while | flops 2727669760 | bytes 159401328 | solution.py:246
  778.2 11.7 fusion.190
  817.6 11.7 fusion.190
  851.9 14.0 convolution_convert_fusion.3
  890.6 14.1 convolution_convert_fusion.2
  905.1 14.1 convolution_convert_fusion.1
  919.3 14.1 convolution_convert_fusion
  937.5 41.7 %reduce-scatter.12.cloned.1.call-done = bf16[256,128]{1,0:T(8,128)(2,1)} async-done(((bf16[2048,128]{1,0:T(8,128)(2,1)}), bf16[256,128]{1,0:T(8,128)(2,1)}) %reduce-scatter.12.cloned.1.call-update) | async-done | bytes 65552 | tf_op jit(solution)/shard_map/reduce_scatter | solution.py:294
  980.7 153.2 %all-reduce.12.cloned.1.call-done = (bf16[1024,2048]{1,0:T(8,128)(2,1)}, bf16[1024,2048]{1,0:T(8,128)(2,1)}) async-done(((bf16[1024,2048]{1,0:T(8,128)(2,1)}, bf16[1024,2048]{1,0:T(8,128)(2,1)}), (bf16[1024,2048]{1,0:T(8,128)(2,1)}, bf16[1024,2048]{1,0:T(8,128)(2,1)})) %all-reduce.12.cloned.1.call-update) | async-done | bytes 8388624 | tf_op jit(solution)/shard_map/psum | solution.py:212
  1139.6 22.3 %all-reduce.2 = (bf16[2048]{0:T(1024)(128)(2,1)S(1)}, bf16[2048]{0:T(1024)(128)(2,1)S(1)}) all-reduce(bf16[2048]{0:T(1024)(128)(2,1)S(1)} %get-tuple-element.132, bf16[2048]{0:T(1024)(128)(2,1)S(1)} %copy-done.43), channel_id=2, replica_groups=mesh['dp'=8,'shard'=4] {'dp'}, use_global_device_ids=true, to_apply=%region_16.17.clone | all-reduce | flops 4096 | bytes 16384
  1163.9 41.8 %reduce-scatter.8.cloned.1.call-done = bf16[256,512]{1,0:T(8,128)(2,1)} async-done(((bf16[2048,512]{1,0:T(8,128)(2,1)}), bf16[256,512]{1,0:T(8,128)(2,1)}) %reduce-scatter.8.cloned.1.call-update) | async-done | bytes 262160 | tf_op jit(solution)/shard_map/reduce_scatter | solution.py:288
  1209.3 67.7 %reduce-scatter.14.cloned.1.call-done = bf16[512,256]{1,0:T(8,128)(2,1)} async-done(((bf16[512,2048]{1,0:T(8,128)(2,1)}), bf16[512,256]{1,0:T(8,128)(2,1)}) %reduce-scatter.14.cloned.1.call-update) | async-done | bytes 262160 | tf_op jit(solution)/shard_map/reduce_scatter | solution.py:297
  1279.3 149.4 %reduce-scatter.16.cloned.1.call-done = bf16[256,2048]{1,0:T(8,128)(2,1)} async-done(((bf16[2048,2048]{1,0:T(8,128)(2,1)}), bf16[256,2048]{1,0:T(8,128)(2,1)}) %reduce-scatter.16.cloned.1.call-update) | async-done | bytes 1048592 | tf_op jit(solution)/shard_map/reduce_scatter | solution.py:303
  1431.8 148.9 %reduce-scatter.18.cloned.1.call-done = bf16[256,2048]{1,0:T(8,128)(2,1)} async-done(((bf16[2048,2048]{1,0:T(8,128)(2,1)}), bf16[256,2048]{1,0:T(8,128)(2,1)}) %reduce-scatter.18.cloned.1.call-update) | async-done | bytes 1048592 | tf_op jit(solution)/shard_map/reduce_scatter | solution.py:306
  1583.7 148.9 %reduce-scatter.20.cloned.1.call-done = bf16[2048,256]{1,0:T(8,128)(2,1)} async-done(((bf16[2048,2048]{1,0:T(8,128)(2,1)}), bf16[2048,256]{1,0:T(8,128)(2,1)}) %reduce-scatter.20.cloned.1.call-update) | async-done | bytes 1048592 | tf_op jit(solution)/shard_map/reduce_scatter | solution.py:309
  1743.7 14.7 fusion.60
  1758.4 20.1 %psum.47 = f32[]{:T(128)} all-reduce(f32[]{:T(128)} %psum.46), channel_id=1, replica_groups=mesh['dp'=8,'shard'=4] {'dp'}, use_global_device_ids=true, to_apply=%region_36.37 | all-reduce | flops 1 | bytes 8 | tf_op jit(solution)/shard_map/psum | solution.py:317
  (262 shorter events, 228.6 us)
Async XLA Ops:
  7.2 103.4 %all-gather.8.cloned.1.call-start = ((), (), s32[]{:S(2)}) async-start(), calls=%async_computation.7 | async-start | bytes 2359296 | tf_op jit(solution)/shard_map/all_gather | solution.py:158
  9.0 138.3 %all-gather.10.cloned.1.call-start = ((), (), s32[]{:S(2)}) async-start(), calls=%async_computation.8 | async-start | bytes 2359296 | tf_op jit(solution)/shard_map/all_gather | solution.py:161
  10.9 226.2 %all-reduce.8.cloned.1.call-start = ((), (), s32[]{:S(2)}) async-start(), calls=%async_computation.9 | async-start | bytes 8388608 | tf_op jit(solution)/shard_map/psum | solution.py:201
  11.0 93.7 %copy-start = (bf16[1024,2048]{1,0:T(8,128)(2,1)S(1)}, bf16[1024,2048]{1,0:T(8,128)(2,1)}, u32[]{:S(2)}) copy-start(bf16[1024,2048]{1,0:T(8,128)(2,1)} %param.27) | copy-start | bytes 12582916
  34.3 72.9 %copy-start.38 = (f32[8,1,256]{2,1,0:T(1,128)}, f32[8,1,256]{2,1,0:T(1,128)S(1)}, u32[]{:S(2)}) copy-start(f32[8,1,256]{2,1,0:T(1,128)S(1)} %convert_element_type.295) | copy-start | bytes 24580
  38.0 71.3 %copy-start.40 = (f32[1024]{0:T(1024)}, f32[1024]{0:T(1024)S(1)}, u32[]{:S(2)}) copy-start(f32[1024]{0:T(1024)S(1)} %get-tuple-element.218) | copy-start | bytes 12292
  71.8 37.5 %copy-start.15 = (bf16[2048,128]{1,0:T(8,128)(2,1)}, bf16[2048,128]{1,0:T(8,128)(2,1)S(1)}, u32[]{:S(2)}) copy-start(bf16[2048,128]{1,0:T(8,128)(2,1)S(1)} %all_gather.28) | copy-start | bytes 1572868
  154.1 210.8 %all-gather.12.cloned.1.call-start = ((), (), s32[]{:S(2)}) async-start(), calls=%async_computation.10 | async-start | bytes 9437184 | tf_op jit(solution)/shard_map/all_gather | solution.py:163
  155.3 335.5 %all-gather.14.cloned.1.call-start = ((), (), s32[]{:S(2)}) async-start(), calls=%async_computation.11 | async-start | bytes 9437184 | tf_op jit(solution)/shard_map/all_gather | solution.py:164
  158.2 458.9 %all-gather.16.cloned.1.call-start = ((), (), s32[]{:S(2)}) async-start(), calls=%async_computation.12 | async-start | bytes 9437184 | tf_op jit(solution)/shard_map/all_gather | solution.py:165
  160.9 589.0 %all-reduce.10.cloned.1.call-start = ((), (), s32[]{:S(2)}) async-start(), calls=%async_computation.13 | async-start | bytes 8388608 | tf_op jit(solution)/shard_map/psum | solution.py:235
  666.1 269.9 %reduce-scatter.10.cloned.1.call-start = ((), (), s32[]{:S(2)}) async-start(), calls=%async_computation.15 | async-start | bytes 589824 | tf_op jit(solution)/shard_map/reduce_scatter | solution.py:291
  767.4 78.9 %copy-start.23 = (f32[1024,32]{0,1:T(8,128)S(1)}, f32[1024,32]{0,1:T(8,128)}, u32[]{:S(2)}) copy-start(f32[1024,32]{0,1:T(8,128)} %copy-done.22) | copy-start | bytes 393220
  767.4 78.9 %copy-start.25 = (f32[1024,32]{0,1:T(8,128)S(1)}, f32[1024,32]{0,1:T(8,128)}, u32[]{:S(2)}) copy-start(f32[1024,32]{0,1:T(8,128)} %copy-done.24) | copy-start | bytes 393220
  851.8 127.5 %reduce-scatter.12.cloned.1.call-start = ((), (), s32[]{:S(2)}) async-start(), calls=%async_computation.16 | async-start | bytes 589824 | tf_op jit(solution)/shard_map/reduce_scatter | solution.py:294
  868.5 265.5 %all-reduce.12.cloned.1.call-start = ((), (), s32[]{:S(2)}) async-start(), calls=%async_computation.21 | async-start | bytes 16777216 | tf_op jit(solution)/shard_map/psum | solution.py:212
  877.1 328.5 %reduce-scatter.8.cloned.1.call-start = ((), (), s32[]{:S(2)}) async-start(), calls=%async_computation.14 | async-start | bytes 2359296 | tf_op jit(solution)/shard_map/reduce_scatter | solution.py:288
  883.4 393.6 %reduce-scatter.14.cloned.1.call-start = ((), (), s32[]{:S(2)}) async-start(), calls=%async_computation.17 | async-start | bytes 2359296 | tf_op jit(solution)/shard_map/reduce_scatter | solution.py:297
  890.5 538.2 %reduce-scatter.16.cloned.1.call-start = ((), (), s32[]{:S(2)}) async-start(), calls=%async_computation.18 | async-start | bytes 9437184 | tf_op jit(solution)/shard_map/reduce_scatter | solution.py:303
  904.7 676.0 %reduce-scatter.18.cloned.1.call-start = ((), (), s32[]{:S(2)}) async-start(), calls=%async_computation.19 | async-start | bytes 9437184 | tf_op jit(solution)/shard_map/reduce_scatter | solution.py:306
  919.3 813.4 %reduce-scatter.20.cloned.1.call-start = ((), (), s32[]{:S(2)}) async-start(), calls=%async_computation.20 | async-start | bytes 9437184 | tf_op jit(solution)/shard_map/reduce_scatter | solution.py:309
  933.4 200.6 %copy-start.39 = (f32[8,1,256]{2,1,0:T(1,128)S(1)}, f32[8,1,256]{2,1,0:T(1,128)}, u32[]{:S(2)}) copy-start(f32[8,1,256]{2,1,0:T(1,128)} %copy-done.38) | copy-start | bytes 24580
  933.4 200.6 %copy-start.41 = (f32[1024]{0:T(1024)S(1)}, f32[1024]{0:T(1024)}, u32[]{:S(2)}) copy-start(f32[1024]{0:T(1024)} %copy-done.40) | copy-start | bytes 12292
  933.4 206.2 %copy-start.43 = (bf16[2048]{0:T(1024)(128)(2,1)S(1)}, bf16[2048]{0:T(1024)(128)(2,1)}, u32[]{:S(2)}) copy-start(bf16[2048]{0:T(1024)(128)(2,1)} %get-tuple-element.130) | copy-start | bytes 12292
  933.4 810.2 %copy-start.42 = (f32[1024]{0:T(1024)S(1)}, f32[1024]{0:T(1024)}, u32[]{:S(2)}) copy-start(f32[1024]{0:T(1024)} %get-tuple-element.217) | copy-start | bytes 12292
  1161.9 581.8 %copy-start.46 = (bf16[2048]{0:T(1024)(128)(2,1)}, bf16[2048]{0:T(1024)(128)(2,1)S(1)}, u32[]{:S(2)}) copy-start(bf16[2048]{0:T(1024)(128)(2,1)S(1)} %get-tuple-element.173) | copy-start | bytes 12292
  1161.9 581.7 %copy-start.47 = (bf16[2048]{0:T(1024)(128)(2,1)}, bf16[2048]{0:T(1024)(128)(2,1)S(1)}, u32[]{:S(2)}) copy-start(bf16[2048]{0:T(1024)(128)(2,1)S(1)} %get-tuple-element.172) | copy-start | bytes 12292
  1743.6 38.5 %copy-start.31 = (bf16[256,512]{1,0:T(8,128)(2,1)S(1)}, bf16[256,512]{1,0:T(8,128)(2,1)}, u32[]{:S(2)}) copy-start(bf16[256,512]{1,0:T(8,128)(2,1)} %reduce-scatter.8.cloned.1.call-done) | copy-start | bytes 786436
  1743.6 40.9 %copy-start.34 = (f32[256,128]{1,0:T(8,128)S(1)}, f32[256,128]{1,0:T(8,128)}, u32[]{:S(2)}) copy-start(f32[256,128]{1,0:T(8,128)} %param.32) | copy-start | bytes 393220
  1743.6 46.5 %copy-start.12 = (f32[256,2048]{1,0:T(8,128)S(1)}, f32[256,2048]{1,0:T(8,128)}, u32[]{:S(2)}) copy-start(f32[256,2048]{1,0:T(8,128)} %param.36) | copy-start | bytes 6291460
  1743.6 46.5 %copy-start.19 = (bf16[256,2048]{1,0:T(8,128)(2,1)S(1)}, bf16[256,2048]{1,0:T(8,128)(2,1)}, u32[]{:S(2)}) copy-start(bf16[256,2048]{1,0:T(8,128)(2,1)} %reduce-scatter.16.cloned.1.call-done) | copy-start | bytes 3145732
  1779.2 15.5 copy-start.13
  (47 other events, 297.0 us)
Sparse Core Ops, SparseCore 0:
  10.7 58.5 all-gather.7
  71.9 52.7 all-gather.9
  154.2 82.7 all-reduce.7
  239.8 125.0 all-gather.11
  367.7 123.0 all-gather.13
  493.4 123.5 all-gather.15
  666.2 83.6 all-reduce.9
  851.9 61.9 reduce-scatter.9
  918.2 61.0 reduce-scatter.11
  981.7 152.2 all-reduce.11
  1138.0 67.5 reduce-scatter.7
  1209.6 67.3 reduce-scatter.13
  1280.6 148.0 reduce-scatter.15
  1432.7 148.0 reduce-scatter.17
  1584.2 148.4 reduce-scatter.19
